TPU v7x, 32 devices: a whole 2x2x4 slice. The times are simulated.
32 devices in a mesh: row: 2 (over y), col: 4 (over x, core), tm: 4 (over z).
Axes of the slice: x: 2, y: 2, z: 4, core: 2. Of those that a mesh axis runs over, the one named last changes fastest.
Arguments:
- filled_orbitals: bfloat16 [4, 1024, 1024], P('col', 'row', 'tm'), may hold values from -0.1875 to 0.1875
- empty_orbitals: bfloat16 [4, 1024, 3072], P('col', 'row', 'tm'), may hold values from -0.109375 to 0.109375
- filled_depth: bfloat16 [1024], P('tm'), may hold values from 0.019897461 to 2
- empty_depth: bfloat16 [3072], P('tm'), may hold values from 0.019897461 to 2
- time_points: float32 [4], P('tm'), may hold values from 0.05 to 8
- cosine_weights: float32 [4, 4], replicated, may hold values from -3 to 3
Outputs:
- polar_freq: float32 [4, 4, 1024, 4096], P(None, None, ('row', 'tm'), 'col')
All inputs are finite; a program needn't handle non-finite values.
Results may differ from a plain program's by a relative error of at most 0.0033.
Values may be sent and summed in bfloat16 or wider, within the bound.
No kernel may reach another device: no remote copies, remote signals or barrier semaphores. Data moves between devices by JAX's collectives and lax.ppermute only.
A program may use at most 128 MiB of HBM per device.

v0:
```python
import jax
import jax.numpy as jnp
from jax import lax
from jax.sharding import PartitionSpec as P


def tile_product(left_points, right_points, depths, tau_value):
    band_count = left_points.shape[-1]
    weight_row = jnp.exp(-depths.astype(jnp.float32) * tau_value)
    scaled = (
        right_points.reshape(-1, band_count).astype(jnp.float32) * weight_row[None, :]
    ).astype(jnp.bfloat16)
    return lax.dot_general(
        left_points.reshape(-1, band_count),
        scaled,
        (((1,), (1,)), ((), ())),
        preferred_element_type=jnp.float32,
    )


def on_device(
    filled_orbitals, empty_orbitals, filled_depth, empty_depth, time_points, cosine_weights
):
    tau_value = time_points[0]
    filled_bands, empty_bands, filled_all, empty_all = (
        lax.all_gather(filled_orbitals, "tm", axis=2, tiled=True),
        lax.all_gather(empty_orbitals, "tm", axis=2, tiled=True),
        lax.all_gather(filled_depth, "tm", axis=0, tiled=True),
        lax.all_gather(empty_depth, "tm", axis=0, tiled=True),
    )
    filled_rows, empty_rows = (
        lax.all_gather(filled_bands, "col", axis=0, tiled=True),
        lax.all_gather(empty_bands, "col", axis=0, tiled=True),
    )
    column_filled, column_empty = lax.all_gather(
        (filled_bands, empty_bands), "row", axis=1, tiled=True
    )
    green_filled = tile_product(filled_rows, column_filled, filled_all, tau_value)
    green_empty = tile_product(empty_rows, column_empty, empty_all, tau_value)
    polar_time = (
        (-(green_filled * green_empty))
        .astype(jnp.bfloat16)
        .reshape(filled_rows.shape[0], filled_rows.shape[1], -1)
    )
    return jnp.einsum(
        "ft,tabc->fabc",
        cosine_weights,
        lax.all_to_all(polar_time[None], "tm", split_axis=2, concat_axis=0, tiled=True).astype(
            jnp.float32
        ),
        precision=lax.Precision.HIGHEST,
    )


def solution(mesh):
    in_specs = (P("col", "row", "tm"), P("col", "row", "tm"), P("tm"), P("tm"), P("tm"), P())
    out_specs = P(None, None, ("row", "tm"), "col")
    return jax.shard_map(
        on_device, mesh=mesh, in_specs=in_specs, out_specs=out_specs, check_vma=False
    )
```

profile of v0, /device:TPU:0, one launch (start us, length us, event | category | flops | bytes accessed | tf_op | source)
XLA Modules:
  0.0 491.7 jit_solution(13205183618008928850)
XLA Ops:
  6.5 0.7 all-gather.15.cloned.1.call-update
  7.3 0.0 all-gather.9.cloned.1.call-start
  7.3 0.7 all-gather.9.cloned.1.call-update
  8.0 0.0 all-gather.17.cloned.1.call-start
  8.1 67.0 %all-gather.15.cloned.1.call-done = bf16[1,512,3072]{2,1,0:T(8,128)(2,1)} async-done(((bf16[1,512,768]{2,1,0:T(8,128)(2,1)}), bf16[1,512,3072]{2,1,0:T(8,128)(2,1)}) %all-gather.15.cloned.1.call-update) | async-done | bytes 3145744 | tf_op jit(solution)/shard_map/all_gather | solution.py:27
  75.1 0.0 all-gather.19.cloned.1.call-start
  75.2 0.5 all-gather.19.cloned.1.call-update
  75.7 0.0 all-gather.11.cloned.1.call-start
  75.8 29.5 %all-gather.9.cloned.1.call-done = bf16[1,512,1024]{2,1,0:T(8,128)(2,1)} async-done(((bf16[1,512,256]{2,1,0:T(8,128)(2,1)}), bf16[1,512,1024]{2,1,0:T(8,128)(2,1)}) %all-gather.9.cloned.1.call-update) | async-done | bytes 1048592 | tf_op jit(solution)/shard_map/all_gather | solution.py:26
  105.3 0.0 all-gather.13.cloned.1.call-start
  105.3 0.5 all-gather.13.cloned.1.call-update
  106.6 10.1 %all-gather = bf16[4,1,256]{2,1,0:T(2,128)(2,1)S(1)} all-gather(bf16[1,1,256]{2,1,0:T(2,128)(2,1)S(1)} %reshape.26), channel_id=1, replica_groups=mesh['row'=2,'col'=4,'tm'=4] {'tm'}, dimensions={0}, use_global_device_ids=true | all-gather | bytes 2560 | tf_op jit(solution)/shard_map/all_gather | solution.py:28
  116.7 13.1 %all-gather.1 = bf16[4,1,768]{2,1,0:T(2,128)(2,1)S(1)} all-gather(bf16[1,1,768]{2,1,0:T(2,128)(2,1)S(1)} %reshape.28), channel_id=1, replica_groups=mesh['row'=2,'col'=4,'tm'=4] {'tm'}, dimensions={0}, use_global_device_ids=true | all-gather | bytes 7680 | tf_op jit(solution)/shard_map/all_gather | solution.py:29
  129.8 55.7 %all-gather.17.cloned.1.call-done = bf16[1,1024,3072]{2,1,0:T(8,128)(2,1)} async-done(((bf16[1,512,3072]{2,1,0:T(8,128)(2,1)}), bf16[1,1024,3072]{2,1,0:T(8,128)(2,1)}) %all-gather.17.cloned.1.call-update) | async-done | bytes 6291472 | tf_op jit(solution)/shard_map/all_gather | solution.py:35
  185.5 83.5 %all-gather.19.cloned.1.call-done = bf16[4,512,3072]{2,1,0:T(8,128)(2,1)} async-done(((bf16[1,512,3072]{2,1,0:T(8,128)(2,1)}), bf16[4,512,3072]{2,1,0:T(8,128)(2,1)}) %all-gather.19.cloned.1.call-update) | async-done | bytes 12582928 | tf_op jit(solution)/shard_map/all_gather | solution.py:33
  269.0 18.9 %fusion.1 = f32[1024,2048]{1,0:T(8,128)} fusion(bf16[2048,3072]{1,0:T(8,128)(2,1)} %bitcast.35, bf16[1,1024,3072]{2,1,0:T(8,128)(2,1)} %all-gather.17.cloned.1.call-done, f32[3072]{0:T(1024)S(1)} %bitcast.33), kind=kOutput, calls=%fused_computation.3 | convolution fusion | flops 12894339072 | bytes 27275264 | tf_op jit(solution)/shard_map/dot_general | solution.py:13
  287.9 15.6 %all-gather.11.cloned.1.call-done = bf16[1,1024,1024]{2,1,0:T(8,128)(2,1)} async-done(((bf16[1,512,1024]{2,1,0:T(8,128)(2,1)}), bf16[1,1024,1024]{2,1,0:T(8,128)(2,1)}) %all-gather.11.cloned.1.call-update) | async-done | bytes 2097168 | tf_op jit(solution)/shard_map/all_gather | solution.py:35
  303.5 35.9 %all-gather.13.cloned.1.call-done = bf16[4,512,1024]{2,1,0:T(8,128)(2,1)} async-done(((bf16[1,512,1024]{2,1,0:T(8,128)(2,1)}), bf16[4,512,1024]{2,1,0:T(8,128)(2,1)}) %all-gather.13.cloned.1.call-update) | async-done | bytes 4194320 | tf_op jit(solution)/shard_map/all_gather | solution.py:32
  339.4 11.8 %fusion.6 = bf16[2048,1024]{0,1:T(8,128)(2,1)} fusion(f32[1024,2048]{1,0:T(8,128)} %fusion.1, bf16[2048,1024]{1,0:T(8,128)(2,1)} %bitcast.36, bf16[1,1024,1024]{2,1,0:T(8,128)(2,1)} %all-gather.11.cloned.1.call-done, f32[1024]{0:T(1024)S(1)} %bitcast.34), kind=kOutput, calls=%fused_computation.9 | convolution fusion | flops 4304404480 | bytes 18878464 | tf_op jit(solution)/shard_map/dot_general | solution.py:13
  351.2 7.8 %broadcast_in_dim_reshape.3 = bf16[1,4,512,1024]{2,1,3,0:T(4,128)(2,1)} reshape(bf16[2048,1024]{0,1:T(8,128)(2,1)} %fusion.6) | data formatting | bytes 8388608 | tf_op jit(solution)/shard_map/broadcast_in_dim;reshape | solution.py:48
  359.0 10.0 %copy.11 = bf16[1,4,512,1024]{3,1,0,2:T(4,128)(2,1)} copy(bf16[1,4,512,1024]{2,1,3,0:T(4,128)(2,1)} %broadcast_in_dim_reshape.3) | data formatting | bytes 8388608 | tf_op jit(solution)/shard_map/broadcast_in_dim;reshape | solution.py:48
  369.0 98.1 %all_to_all.18 = bf16[1,4,512,1024]{3,1,0,2:T(4,128)(2,1)S(1)} all-to-all(bf16[1,4,512,1024]{3,1,0,2:T(4,128)(2,1)} %copy.11), channel_id=1, replica_groups=mesh['row'=2,'col'=4,'tm'=4] {'tm'}, dimensions={2} | all-to-all | bytes 8388608 | tf_op jit(solution)/shard_map/all_to_all | solution.py:48
  467.2 9.4 %convolution_bitcast_fusion = f32[4,4,128,1024]{3,0,2,1:T(4,128)S(1)} fusion(bf16[1,4,4,128,1024]{4,1,3,2,0:T(4,128)(2,1)S(1)} %bitcast.32, f32[4,4]{1,0:T(4,128)S(1)} %copy-done), kind=kOutput, calls=%fused_computation.5 | convolution fusion | flops 100663296 | bytes 12582976 | tf_op jit(solution)/shard_map/ft,tabc->fabc/dot_general | solution.py:45
  476.6 8.3 %copy.14 = f32[4,4,128,1024]{3,2,1,0:T(8,128)} copy(f32[4,4,128,1024]{3,0,2,1:T(4,128)S(1)} %convolution_bitcast_fusion) | data formatting | bytes 16777216 | tf_op jit(solution)/shard_map/ft,tabc->fabc/dot_general | solution.py:45
  (13 shorter events, 0.1 us)
Async XLA Ops:
  6.5 460.6 %copy-start = (f32[4,4]{1,0:T(4,128)S(1)}, f32[4,4]{1,0:T(4,128)}, u32[]{:S(2)}) copy-start(f32[4,4]{1,0:T(4,128)} %param.11) | copy-start | bytes 196
  6.5 68.6 %all-gather.15.cloned.1.call-start = ((), (), s32[]{:S(2)}) async-start(), calls=%async_computation.4 | async-start | bytes 3932160 | tf_op jit(solution)/shard_map/all_gather | solution.py:27
  7.3 98.0 %all-gather.9.cloned.1.call-start = ((), (), s32[]{:S(2)}) async-start(), calls=%async_computation.1 | async-start | bytes 1310720 | tf_op jit(solution)/shard_map/all_gather | solution.py:26
  8.0 177.5 %all-gather.17.cloned.1.call-start = ((), (), s32[]{:S(2)}) async-start(), calls=%async_computation.5 | async-start | bytes 9437184 | tf_op jit(solution)/shard_map/all_gather | solution.py:35
  75.1 31.4 %copy-start.1 = (bf16[768]{0:T(1024)(128)(2,1)S(1)}, bf16[768]{0:T(1024)(128)(2,1)}, u32[]{:S(2)}) copy-start(bf16[768]{0:T(1024)(128)(2,1)} %param.9) | copy-start | bytes 4612
  75.1 31.4 %copy-start.2 = (bf16[256]{0:T(256)(128)(2,1)S(1)}, bf16[256]{0:T(256)(128)(2,1)}, u32[]{:S(2)}) copy-start(bf16[256]{0:T(256)(128)(2,1)} %param.8) | copy-start | bytes 1540
  75.1 193.9 %all-gather.19.cloned.1.call-start = ((), (), s32[]{:S(2)}) async-start(), calls=%async_computation.6 | async-start | bytes 15728640 | tf_op jit(solution)/shard_map/all_gather | solution.py:33
  75.7 227.8 %all-gather.11.cloned.1.call-start = ((), (), s32[]{:S(2)}) async-start(), calls=%async_computation.2 | async-start | bytes 3145728 | tf_op jit(solution)/shard_map/all_gather | solution.py:35
  105.3 234.2 %all-gather.13.cloned.1.call-start = ((), (), s32[]{:S(2)}) async-start(), calls=%async_computation.3 | async-start | bytes 5242880 | tf_op jit(solution)/shard_map/all_gather | solution.py:32
Sparse Core Ops, SparseCore 0:
  8.9 66.1 all-gather.14
  76.7 28.5 all-gather.8
  106.8 78.6 all-gather.16
  186.9 82.0 all-gather.18
  270.4 33.0 all-gather.10
  305.0 34.4 all-gather.12
where the time goes:
time: 492 us
  waiting for transfers between devices  290 us (59%)
  blocking collectives  121 us (25%)
  matrix products  40.1 us (8%)
  local copies, waits for them, and re-layouts  26.1 us (5%)
  between operations  14.2 us (3%)
    all_to_all x1, blocking collectives, on_device(): lax.all_to_all(polar_time[None], 'tm', split_axis=2, concat_axis=0, tiled...  98.1 us
    all_gather x1, waiting for transfers between devices, on_device(): lax.all_gather(empty_bands, 'col', axis=0, tiled=True)  83.5 us
    all_gather x2, waiting for transfers between devices, on_device(): lax.all_gather((filled_bands, empty_bands), 'row', axis=1, tiled=True)  71.3 us
    all_gather x1, waiting for transfers between devices, on_device(): lax.all_gather(empty_orbitals, 'tm', axis=2, tiled=True)  67 us
    all_gather x1, waiting for transfers between devices, on_device(): lax.all_gather(filled_bands, 'col', axis=0, tiled=True)  35.9 us
    dot_general x2, matrix products, tile_product(): lax.dot_general(left_points.reshape(-1, band_count), scaled, (((1,), (1,)...  30.6 us
    all_gather x1, waiting for transfers between devices, on_device(): lax.all_gather(filled_orbitals, 'tm', axis=2, tiled=True)  29.5 us
    another operation x2, local copies, waits for them, and re-layouts, on_device(): polar_time[None]  17.8 us
  transfers between devices with their start and end apart: 6, of which 6 were waited for; matrix products, arithmetic and copies ran while one was open for 4% of the time, Pallas kernels for 0%

commit v1 on v0

--- a/solution.py
+++ b/solution.py
@@ -2,6 +2,7 @@
 import jax.numpy as jnp
 from jax import lax
 from jax.sharding import PartitionSpec as P
+from jax.lax import axis_index, axis_size, ppermute
 
 
 def tile_product(left_points, right_points, depths, tau_value):
@@ -21,6 +22,22 @@
 def on_device(
     filled_orbitals, empty_orbitals, filled_depth, empty_depth, time_points, cosine_weights
 ):
+
+    def convert_racks_here(t0, mesh_ax):
+        chips = axis_size(mesh_ax)
+        vals = [(ix, (ix + 1) % chips) for ix in range(chips)]
+        back, t_next = ([t0], [t0])
+        crops = [(ix, (ix - 1) % chips) for ix in range(chips)]
+        for _ in range(chips // 2):
+            everything = ppermute(back[-1], mesh_ax, vals)
+            back.append(everything)
+        for _ in range((chips - 1) // 2):
+            local_now = ppermute(t_next[-1], mesh_ax, crops)
+            t_next.append(local_now)
+        moved = jnp.concatenate([*back[::-1], *t_next[1:]], axis=0)
+        local_part = axis_index(mesh_ax)
+        return jnp.roll(moved, (local_part - chips // 2) * t0.shape[0], 0)
+
     tau_value = time_points[0]
     filled_bands, empty_bands, filled_all, empty_all = (
         lax.all_gather(filled_orbitals, "tm", axis=2, tiled=True),
@@ -29,7 +46,7 @@
         lax.all_gather(empty_depth, "tm", axis=0, tiled=True),
     )
     filled_rows, empty_rows = (
-        lax.all_gather(filled_bands, "col", axis=0, tiled=True),
+        convert_racks_here(filled_bands, mesh_ax="col"),
         lax.all_gather(empty_bands, "col", axis=0, tiled=True),
     )
     column_filled, column_empty = lax.all_gather(

time: 492 us -> 439 us (0.89)
  waiting for transfers between devices: 290 us -> 244 us
  local copies, waits for them, and re-layouts: 26.1 us -> 19.6 us
    all_gather x1 -> x0, waiting for transfers between devices: 35.9 us -> none  [on_device(): lax.all_gather(filled_bands, 'col', axis=0, tiled=True)]
    all_gather x2, waiting for transfers between devices: 71.3 us -> 47.1 us  [on_device(): lax.all_gather((filled_bands, empty_bands), 'row', axis=1, tiled=True)]
    another operation x2 -> x1, local copies, waits for them, and re-layouts: 17.8 us -> 3.24 us  [on_device(): polar_time[None]]
    ppermute x0 -> x3, waiting for transfers between devices: none -> 14.4 us  [the longest x2 14.4 us: convert_racks_here(): everything = ppermute(back[-1], mesh_ax, vals)]
    unnamed x8 -> x13, local copies, waits for them, and re-layouts: 0.02 us -> 5.52 us
  transfers between devices with their start and end apart: 6 -> 8, of which waited for: 6 -> 6; matrix products, arithmetic and copies ran while one was open for 4% -> 6% of each run, Pallas kernels for 0% -> 0%
where the time goes in v1:
time: 439 us; the launch traced here: 438 us
  waiting for transfers between devices  244 us (56%)
  blocking collectives  121 us (28%)
  matrix products  38.6 us (9%)
  local copies, waits for them, and re-layouts  19.6 us (4%)
  between operations  13.9 us (3%)
    all_to_all x1, blocking collectives, on_device(): lax.all_to_all(polar_time[None], 'tm', split_axis=2, concat_axis=0, tiled...  97.4 us
    all_gather x1, waiting for transfers between devices, on_device(): lax.all_gather(empty_bands, 'col', axis=0, tiled=True)  83.5 us
    all_gather x1, waiting for transfers between devices, on_device(): lax.all_gather(empty_orbitals, 'tm', axis=2, tiled=True)  67 us
    all_gather x2, waiting for transfers between devices, on_device(): lax.all_gather((filled_bands, empty_bands), 'row', axis=1, tiled=True)  47.1 us
    all_gather x1, waiting for transfers between devices, on_device(): lax.all_gather(filled_orbitals, 'tm', axis=2, tiled=True)  29.5 us
    dot_general x2, matrix products, tile_product(): lax.dot_general(left_points.reshape(-1, band_count), scaled, (((1,), (1,)...  29.2 us
    ppermute x2, waiting for transfers between devices, convert_racks_here(): everything = ppermute(back[-1], mesh_ax, vals)  14.4 us
    all_gather x1, blocking collectives, on_device(): lax.all_gather(empty_depth, 'tm', axis=0, tiled=True)  13.1 us
  transfers between devices with their start and end apart: 8, of which 6 were waited for; matrix products, arithmetic and copies ran while one was open for 6% of the time, Pallas kernels for 0%

profile of v1, /device:TPU:0, one launch (start us, length us, event | category | flops | bytes accessed | tf_op | source)
XLA Modules:
  0.0 438.2 jit_solution(13781520922988406546)
XLA Ops:
  6.5 0.7 all-gather.12.cloned.1.call-update
  7.3 0.7 all-gather.8.cloned.1.call-update
  8.1 67.0 %all-gather.12.cloned.1.call-done = bf16[1,512,3072]{2,1,0:T(8,128)(2,1)} async-done(((bf16[1,512,768]{2,1,0:T(8,128)(2,1)}), bf16[1,512,3072]{2,1,0:T(8,128)(2,1)}) %all-gather.12.cloned.1.call-update) | async-done | bytes 3145744 | tf_op jit(solution)/shard_map/all_gather | solution.py:44
  75.2 0.5 all-gather.16.cloned.1.call-update
  75.7 29.5 %all-gather.8.cloned.1.call-done = bf16[1,512,1024]{2,1,0:T(8,128)(2,1)} async-done(((bf16[1,512,256]{2,1,0:T(8,128)(2,1)}), bf16[1,512,1024]{2,1,0:T(8,128)(2,1)}) %all-gather.8.cloned.1.call-update) | async-done | bytes 1048592 | tf_op jit(solution)/shard_map/all_gather | solution.py:43
  105.3 14.4 %collective-permute-done = bf16[1,512,1024]{2,1,0:T(8,128)(2,1)S(1)} collective-permute-done((bf16[1,512,1024]{2,1,0:T(8,128)(2,1)}, bf16[1,512,1024]{2,1,0:T(8,128)(2,1)S(1)}, u32[]{:S(2)}, u32[]{:S(2)}) %collective-permute-start) | collective-permute-done | bytes 1048608 | tf_op jit(solution)/shard_map/ppermute | solution.py:32
  119.7 1.7 collective-permute-start.2
  121.4 0.7 reshape.28
  122.8 0.7 reshape.26
  123.5 10.1 %all-gather = bf16[4,1,256]{2,1,0:T(2,128)(2,1)S(1)} all-gather(bf16[1,1,256]{2,1,0:T(2,128)(2,1)S(1)} %reshape.26), channel_id=1, replica_groups=mesh['row'=2,'col'=4,'tm'=4] {'tm'}, dimensions={0}, use_global_device_ids=true | all-gather | bytes 2560 | tf_op jit(solution)/shard_map/all_gather | solution.py:45
  133.6 13.1 %all-gather.1 = bf16[4,1,768]{2,1,0:T(2,128)(2,1)S(1)} all-gather(bf16[1,1,768]{2,1,0:T(2,128)(2,1)S(1)} %reshape.28), channel_id=1, replica_groups=mesh['row'=2,'col'=4,'tm'=4] {'tm'}, dimensions={0}, use_global_device_ids=true | all-gather | bytes 7680 | tf_op jit(solution)/shard_map/all_gather | solution.py:46
  146.8 1.3 constant_dynamic-update-slice_fusion.7
  148.1 1.3 constant_dynamic-update-slice_fusion.5
  149.5 1.3 constant_dynamic-update-slice_fusion.3
  151.1 2.5 constant_dynamic-slice_fusion
  153.6 31.9 %all-gather.14.cloned.1.call-done = bf16[1,1024,3072]{2,1,0:T(8,128)(2,1)} async-done(((bf16[1,512,3072]{2,1,0:T(8,128)(2,1)}), bf16[1,1024,3072]{2,1,0:T(8,128)(2,1)}) %all-gather.14.cloned.1.call-update) | async-done | bytes 6291472 | tf_op jit(solution)/shard_map/all_gather | solution.py:52
  185.5 83.5 %all-gather.16.cloned.1.call-done = bf16[4,512,3072]{2,1,0:T(8,128)(2,1)} async-done(((bf16[1,512,3072]{2,1,0:T(8,128)(2,1)}), bf16[4,512,3072]{2,1,0:T(8,128)(2,1)}) %all-gather.16.cloned.1.call-update) | async-done | bytes 12582928 | tf_op jit(solution)/shard_map/all_gather | solution.py:50
  269.0 19.4 %fusion.3 = f32[1024,2048]{0,1:T(8,128)} fusion(bf16[2048,3072]{1,0:T(8,128)(2,1)} %bitcast.40, bf16[1,1024,3072]{2,1,0:T(8,128)(2,1)} %all-gather.14.cloned.1.call-done, f32[3072]{0:T(1024)S(1)} %bitcast.38), kind=kOutput, calls=%fused_computation.5 | convolution fusion | flops 12894339072 | bytes 27275264 | tf_op jit(solution)/shard_map/dot_general | solution.py:14
  288.4 15.2 %all-gather.10.cloned.1.call-done = bf16[1,1024,1024]{2,1,0:T(8,128)(2,1)} async-done(((bf16[1,512,1024]{2,1,0:T(8,128)(2,1)}), bf16[1,1024,1024]{2,1,0:T(8,128)(2,1)}) %all-gather.10.cloned.1.call-update) | async-done | bytes 2097168 | tf_op jit(solution)/shard_map/all_gather | solution.py:52
  303.5 9.8 %fusion.1 = bf16[2048,1024]{1,0:T(8,128)(2,1)S(1)} fusion(f32[1024,2048]{0,1:T(8,128)} %fusion.3, bf16[2048,1024]{1,0:T(8,128)(2,1)} %bitcast.36, bf16[1,1024,1024]{2,1,0:T(8,128)(2,1)} %all-gather.10.cloned.1.call-done, f32[1024]{0:T(1024)S(1)} %bitcast.39), kind=kOutput, calls=%fused_computation.3 | convolution fusion | flops 4304404480 | bytes 18878464 | tf_op jit(solution)/shard_map/dot_general | solution.py:14
  313.4 3.2 copy.13
  316.6 97.4 %all_to_all.18 = bf16[1,4,512,1024]{3,1,0,2:T(4,128)(2,1)S(1)} all-to-all(bf16[1,4,512,1024]{3,1,0,2:T(4,128)(2,1)S(1)} %copy.13), channel_id=1, replica_groups=mesh['row'=2,'col'=4,'tm'=4] {'tm'}, dimensions={2} | all-to-all | bytes 8388608 | tf_op jit(solution)/shard_map/all_to_all | solution.py:65
  414.0 9.4 %convolution_bitcast_fusion = f32[4,4,128,1024]{3,0,2,1:T(4,128)S(1)} fusion(bf16[1,4,4,128,1024]{4,1,3,2,0:T(4,128)(2,1)S(1)} %bitcast.35, f32[4,4]{1,0:T(4,128)S(1)} %copy-done), kind=kOutput, calls=%fused_computation.7 | convolution fusion | flops 100663296 | bytes 12582976 | tf_op jit(solution)/shard_map/ft,tabc->fabc/dot_general | solution.py:62
  423.5 8.3 %copy.16 = f32[4,4,128,1024]{3,2,1,0:T(8,128)} copy(f32[4,4,128,1024]{3,0,2,1:T(4,128)S(1)} %convolution_bitcast_fusion) | data formatting | bytes 16777216 | tf_op jit(solution)/shard_map/ft,tabc->fabc/dot_general | solution.py:62
  (22 shorter events, 0.6 us)
Async XLA Ops:
  6.5 407.5 %copy-start = (f32[4,4]{1,0:T(4,128)S(1)}, f32[4,4]{1,0:T(4,128)}, u32[]{:S(2)}) copy-start(f32[4,4]{1,0:T(4,128)} %param.11) | copy-start | bytes 196
  6.5 68.6 %all-gather.12.cloned.1.call-start = ((), (), s32[]{:S(2)}) async-start(), calls=%async_computation.3 | async-start | bytes 3932160 | tf_op jit(solution)/shard_map/all_gather | solution.py:44
  7.3 98.0 %all-gather.8.cloned.1.call-start = ((), (), s32[]{:S(2)}) async-start(), calls=%async_computation.1 | async-start | bytes 1310720 | tf_op jit(solution)/shard_map/all_gather | solution.py:43
  8.0 177.5 %all-gather.14.cloned.1.call-start = ((), (), s32[]{:S(2)}) async-start(), calls=%async_computation.4 | async-start | bytes 9437184 | tf_op jit(solution)/shard_map/all_gather | solution.py:52
  75.1 193.9 %all-gather.16.cloned.1.call-start = ((), (), s32[]{:S(2)}) async-start(), calls=%async_computation.5 | async-start | bytes 15728640 | tf_op jit(solution)/shard_map/all_gather | solution.py:50
  75.7 227.8 %all-gather.10.cloned.1.call-start = ((), (), s32[]{:S(2)}) async-start(), calls=%async_computation.2 | async-start | bytes 3145728 | tf_op jit(solution)/shard_map/all_gather | solution.py:52
  105.3 45.6 %copy-start.1 = (bf16[1,512,1024]{2,1,0:T(8,128)(2,1)S(1)}, bf16[1,512,1024]{2,1,0:T(8,128)(2,1)}, u32[]{:S(2)}) copy-start(bf16[1,512,1024]{2,1,0:T(8,128)(2,1)} %all-gather.8.cloned.1.call-done) | copy-start | bytes 3145732
  105.3 14.4 %collective-permute-start = (bf16[1,512,1024]{2,1,0:T(8,128)(2,1)}, bf16[1,512,1024]{2,1,0:T(8,128)(2,1)S(1)}, u32[]{:S(2)}, u32[]{:S(2)}) collective-permute-start(bf16[1,512,1024]{2,1,0:T(8,128)(2,1)} %all-gather.8.cloned.1.call-done), channel_id=1, source_target_pairs={{0,4},{4,8},{8,12},{12,0},{1,5},{5,9},{9,13},{13,1},{2,6},{6,10},{... | collective-permute-start | bytes 3145736 | tf_op jit(solution)/shard_map/ppermute | solution.py:32
  119.7 27.1 %collective-permute-start.1 = (bf16[1,512,1024]{2,1,0:T(8,128)(2,1)S(1)}, bf16[1,512,1024]{2,1,0:T(8,128)(2,1)}, u32[]{:S(2)}, u32[]{:S(2)}) collective-permute-start(bf16[1,512,1024]{2,1,0:T(8,128)(2,1)S(1)} %collective-permute-done), channel_id=1, source_target_pairs={{0,4},{4,8},{8,12},{12,0},{1,5},{5,9},{9,13},{13,1},{2,6},{6,10},{... | collective-permute-start | bytes 3145736 | tf_op jit(solution)/shard_map/ppermute | solution.py:32
  119.7 29.7 %collective-permute-start.2 = (bf16[1,512,1024]{2,1,0:T(8,128)(2,1)}, bf16[1,512,1024]{2,1,0:T(8,128)(2,1)S(1)}, u32[]{:S(2)}, u32[]{:S(2)}) collective-permute-start(bf16[1,512,1024]{2,1,0:T(8,128)(2,1)} %all-gather.8.cloned.1.call-done), channel_id=1, source_target_pairs={{0,12},{4,0},{8,4},{12,8},{1,13},{5,1},{9,5},{13,9},{2,14},{6,2},{... | collective-permute-start | bytes 3145736 | tf_op jit(solution)/shard_map/ppermute | solution.py:35
Sparse Core Ops, SparseCore 0:
  8.9 66.1 all-gather.11
  76.7 28.5 all-gather.7
  106.8 78.6 all-gather.13
  186.9 82.0 all-gather.15
  270.4 33.0 all-gather.9
